TPU v7x, 32 devices: a whole 2x2x4 slice. The times are simulated.
32 devices in a mesh: groups: 2 (over y), seq: 4 (over z), section: 2 (over x), chan: 2 (over core).
Axes of the slice: x: 2, y: 2, z: 4, core: 2. Of those that a mesh axis runs over, the one named last changes fastest.
Arguments:
- base_codes: int32 [131072], P(('groups', 'seq', 'section')), parts along dimension 0, may hold values from 0 to 3
- stem_weight: bfloat16 [64, 768], replicated, as said below
- conv_gain: float32 [768], replicated, may hold values from 0.1 to 1.9
- dilated_conv_weight: bfloat16 [3, 768, 768], P(None, None, 'chan'), may hold values from -0.125 to 0.125
- widen_weight: bfloat16 [768, 1536], P(None, 'chan'), may hold values from -0.21875 to 0.21875
- token_gain: float32 [1536], replicated, may hold values from 0.1 to 1.9
- proj_weight: bfloat16 [1536, 256], replicated, may hold values from -0.15625 to 0.15625
- dist_weight: float32 [128], replicated, may hold values from -4 to 4
- pair_weight_one: bfloat16 [3, 3, 128, 128], P(None, None, None, 'chan'), may hold values from -0.1875 to 0.1875
- pair_weight_two: bfloat16 [3, 3, 128, 128], P(None, None, None, 'chan'), may hold values from -0.1875 to 0.1875
Outputs:
- fine_features: bfloat16 [4096, 1536], P(('groups', 'seq', 'section'), 'chan'), parts along dimension 0
- pair_map: bfloat16 [128, 64, 32], P('chan', ('groups', 'seq'), 'section'), parts along dimension 1
There are 2 independent parts, one for each index of `groups`. A program takes and returns all parts, laid end to end along the dimension named above; an argument that names none is the same for every part. Nothing has to cross between parts.
Inputs may be any that keep to these rules, and one draw needn't show every extreme that they name: Each entry of stem_weight is under 9 / sqrt(16) in magnitude.
All inputs are finite; a program needn't handle non-finite values.
Results may differ from a plain program's by a relative error of at most 0.015.
Values may be sent and summed in bfloat16 or wider, within the bound.
No kernel may reach another device: no remote copies, remote signals or barrier semaphores. Data moves between devices by JAX's collectives and lax.ppermute only.
A program may use at most 64 MiB of HBM per device.

v0:
```python
import functools
import math

import jax
import jax.numpy as jnp
from jax import lax
from jax.experimental import pallas as pl
from jax.experimental.pallas import tpu as pltpu
from jax.sharding import PartitionSpec as P


PC = 128
PATCH = 16
POOL = 64
DILATION_ROWS = 4


epsilon = 1e-06
LANES = 128
SUB = 8
CHIPS = ("seq", "section")
ALL = ("groups", "seq", "section", "chan")
VMEM = pl.BlockSpec(memory_space=pltpu.VMEM)
SMEM = pl.BlockSpec(memory_space=pltpu.SMEM)
HBM = pl.BlockSpec(memory_space=pltpu.HBM)
ANY = pl.BlockSpec(memory_space=pl.ANY)
LIMIT = 16 << 20


def swap(values):
    count = lax.axis_size("chan")
    return lax.ppermute(values, "chan", [(i, count - 1 - i) for i in range(count)])


def dot(a, b):
    return jnp.dot(a, b, preferred_element_type=jnp.float32)


def iota(shape, axis):
    return lax.broadcasted_iota(jnp.int32, shape, axis)


def spread_codes(tiles):
    own_patch = iota((SUB, LANES), 1) // PATCH == iota((SUB, LANES), 0)
    picked = jnp.concatenate(
        [jnp.where(own_patch, t, 0).astype(jnp.float32) for t in tiles], axis=0
    ).astype(jnp.bfloat16)
    width = 4 * PATCH
    gather = (iota((LANES, width), 0) % PATCH == iota((LANES, width), 1) // 4).astype(jnp.bfloat16)
    return dot(picked, gather)


def stem_of(codes, valid, stem_weight, gain):
    base = (iota(codes.shape, 1) % 4).astype(jnp.float32)
    onehot = jnp.where((codes == base) & valid, 1.0, 0.0).astype(jnp.bfloat16)
    stem = dot(onehot, stem_weight).astype(jnp.bfloat16).astype(jnp.float32)
    mean_square = jnp.mean(stem * stem, axis=1, keepdims=True)
    normed = (stem * lax.rsqrt(mean_square + epsilon) * gain).astype(jnp.bfloat16)
    return stem, normed


def in_lanes(rows):
    return jnp.concatenate([rows[r : r + 1] for r in range(rows.shape[0])], axis=1)


def taps_of(normed, weight_ref, sum_ref, rows):
    first = dot(normed, weight_ref[0])
    centre = dot(normed, weight_ref[1])
    third = dot(normed, weight_ref[2])
    sum_ref[...] = first[: rows + SUB] + third[SUB:]
    return centre[SUB : SUB + rows] + sum_ref[DILATION_ROWS : DILATION_ROWS + rows]


def stem_kernel(
    place_ref,
    codes_hbm,
    stem_weight_hbm,
    conv_gain_hbm,
    dilated_hbm,
    widen_hbm,
    token_gain_hbm,
    proj_hbm,
    stem_ref,
    normed_ref,
    taps_ref,
    edge_weight_ref,
    stem_weight_ref,
    conv_gain_ref,
    widen_ref,
    token_gain_ref,
    proj_ref,
    codes_ref,
    near_ref,
    dilated_ref,
    sum_ref,
    sems,
):
    copies = [
        pltpu.make_async_copy(source, target, sems.at[n])
        for n, (source, target) in enumerate(
            (
                (codes_hbm, codes_ref),
                (stem_weight_hbm, stem_weight_ref),
                (conv_gain_hbm, conv_gain_ref),
                (dilated_hbm, dilated_ref),
                (widen_hbm, widen_ref),
                (token_gain_hbm, token_gain_ref),
                (proj_hbm, proj_ref),
            )
        )
    ]
    for copy in copies:
        copy.start()
    core = place_ref[0]
    code_rows = codes_ref.shape[0] // 2
    rows = code_rows * SUB
    ext = rows + 2 * SUB
    for copy in copies[:3]:
        copy.wait()
    own = jnp.where(core == 0, codes_ref[:code_rows], codes_ref[code_rows:])
    near_ref[SUB : SUB + code_rows] = own
    near_ref[0:SUB] = codes_ref[code_rows - SUB : code_rows]
    near_ref[SUB + code_rows : 2 * SUB + code_rows] = codes_ref[code_rows : code_rows + SUB]
    tiles = [
        near_ref[pl.ds(SUB - 1 + r, SUB, stride=0), :] for r in range(code_rows + 2)
    ]
    row = iota((ext, 4 * PATCH), 0)
    valid = ((row >= SUB) | (core > 0)) & ((row < ext - SUB) | (core == 0))
    stem, normed = stem_of(
        spread_codes(tiles), valid, stem_weight_ref[...], in_lanes(conv_gain_ref[...])
    )
    stem_ref[...] = stem[SUB : SUB + rows].astype(jnp.bfloat16)
    normed_ref[...] = normed
    copies[3].wait()
    taps_ref[...] = taps_of(normed, dilated_ref, sum_ref, rows)
    edge_weight_ref[...] = dilated_ref[2 * core]
    for copy in copies[4:]:
        copy.wait()


def stem_call(place, codes, stem_weight, conv_gain, dilated, widen, token_gain, proj):
    channels = stem_weight.shape[1]
    half = dilated.shape[2]
    rows = codes.shape[0] // 2 * SUB
    shape = jax.ShapeDtypeStruct
    out_shape = (
        shape((rows, channels), jnp.bfloat16),
        shape((rows + 2 * SUB, channels), jnp.bfloat16),
        shape((rows, half), jnp.float32),
        shape((channels, half), jnp.bfloat16),
        shape(stem_weight.shape, jnp.bfloat16),
        shape(conv_gain.shape, jnp.float32),
        shape(widen.shape, jnp.bfloat16),
        shape(token_gain.shape, jnp.float32),
        shape(proj.shape, jnp.bfloat16),
    )
    return pl.pallas_call(
        stem_kernel,
        out_shape=out_shape,
        in_specs=[SMEM] + [HBM] * 7,
        out_specs=(VMEM,) * len(out_shape),
        scratch_shapes=[
            pltpu.VMEM(codes.shape, jnp.int32),
            pltpu.VMEM((codes.shape[0] // 2 + 3 * SUB, LANES), jnp.int32),
            pltpu.VMEM(dilated.shape, jnp.bfloat16),
            pltpu.VMEM((rows + SUB, half), jnp.float32),
            pltpu.SemaphoreType.DMA((7,)),
        ],
        compiler_params=pltpu.CompilerParams(vmem_limit_bytes=LIMIT),
        cost_estimate=pl.CostEstimate(
            flops=6 * rows * channels * half, bytes_accessed=4 << 20, transcendentals=0
        ),
        name="stem",
    )(place, codes, stem_weight, conv_gain, dilated, widen, token_gain, proj)


def tower_kernel(
    place_ref,
    received_ref,
    stem_ref,
    normed_ref,
    taps_ref,
    edge_weight_ref,
    stem_weight_ref,
    conv_gain_ref,
    dilated_ref,
    halved_ref,
    near_ref,
    sum_ref,
    tower_ref,
):
    core, outside = place_ref[0], place_ref[1]
    rows = stem_ref.shape[0]
    half = taps_ref.shape[1]
    end = received_ref.shape[0]
    near_ref[0:SUB] = jnp.where(core == 0, received_ref[end - SUB :], received_ref[:SUB])
    near_ref[SUB:] = jnp.zeros((SUB, LANES), jnp.int32)
    tile = jnp.where(
        core == 0,
        near_ref[pl.ds(SUB - 1, SUB, stride=0), :],
        near_ref[pl.ds(0, SUB, stride=0), :],
    )
    _, edge = stem_of(
        spread_codes([tile]), outside > 0, stem_weight_ref[...], in_lanes(conv_gain_ref[...])
    )
    other_taps = taps_of(normed_ref[...], dilated_ref, sum_ref, rows)
    for taps, edge_weight, which in (
        (taps_ref[...], edge_weight_ref[...], core),
        (other_taps, dilated_ref[2 * core], 1 - core),
    ):
        added = pltpu.roll(dot(edge, edge_weight), DILATION_ROWS, 0)
        row = iota(added.shape, 0)
        head = jnp.where((row < DILATION_ROWS) & (core == 0), added, 0.0)
        tail = jnp.where((row >= DILATION_ROWS) & (core > 0), added, 0.0)
        taps = jnp.concatenate(
            [taps[:SUB] + head, taps[SUB : rows - SUB], taps[rows - SUB :] + tail], axis=0
        )
        columns = pl.ds(pl.multiple_of(which * half, LANES), half)
        tower = stem_ref[:, columns].astype(jnp.float32) + jax.nn.gelu(taps)
        pooled = []
        for c in range(half // LANES):
            tower_ref[c] = tower[:, c * LANES : (c + 1) * LANES]
            even = tower_ref[c, pl.ds(0, rows // 2, stride=2), :]
            odd = tower_ref[c, pl.ds(1, rows // 2, stride=2), :]
            pooled.append(jnp.maximum(even, odd))
        halved_ref[:, columns] = jnp.concatenate(pooled, axis=1).astype(jnp.bfloat16)


def tower_call(place, received, stem, normed, taps, edge_weight, stem_weight, conv_gain, dilated):
    rows, channels = stem.shape
    half = taps.shape[1]
    return pl.pallas_call(
        tower_kernel,
        out_shape=jax.ShapeDtypeStruct((rows // 2, channels), jnp.bfloat16),
        in_specs=[SMEM] + [VMEM] * 8,
        out_specs=VMEM,
        scratch_shapes=[
            pltpu.VMEM((2 * SUB, LANES), jnp.int32),
            pltpu.VMEM((rows + SUB, half), jnp.float32),
            pltpu.VMEM((half // LANES, rows, LANES), jnp.float32),
        ],
        compiler_params=pltpu.CompilerParams(vmem_limit_bytes=LIMIT),
        cost_estimate=pl.CostEstimate(
            flops=6 * rows * channels * half,
            bytes_accessed=4 << 20,
            transcendentals=rows * channels,
        ),
        name="tower",
    )(place, received, stem, normed, taps, edge_weight, stem_weight, conv_gain, dilated)


def widen_kernel(
    place_ref,
    halved_ref,
    widen_ref,
    widen_other_ref,
    token_gain_ref,
    proj_ref,
    fine_ref,
    fine_other_ref,
    spread_ref,
):
    core = place_ref[0]
    halved = halved_ref[...]
    token_count = halved.shape[0] // POOL
    tokens = []
    for weight_ref, out_ref in ((widen_ref, fine_ref), (widen_other_ref, fine_other_ref)):
        fine = jax.nn.gelu(dot(halved, weight_ref[...])).astype(jnp.bfloat16)
        out_ref[...] = fine
        fine = fine.astype(jnp.float32)
        tokens.append(
            jnp.concatenate(
                [
                    jnp.mean(fine[t * POOL : (t + 1) * POOL], axis=0, keepdims=True)
                    for t in range(token_count)
                ],
                axis=0,
            )
            .astype(jnp.bfloat16)
            .astype(jnp.float32)
        )
    wide = widen_ref.shape[1]
    squares = sum(jnp.sum(t * t, axis=1, keepdims=True) for t in tokens)
    scale = lax.rsqrt(squares / (2 * wide) + epsilon)
    gain = token_gain_ref[...]
    gain_rows = wide // LANES
    gains = [in_lanes(gain[:gain_rows]), in_lanes(gain[gain_rows:])]
    factors = 0.0
    for token, which in zip(tokens, (core, 1 - core)):
        start = pl.multiple_of(which * wide, LANES)
        gain = jnp.where(which == 0, gains[0], gains[1])
        factors = factors + dot(
            (token * scale * gain).astype(jnp.bfloat16), proj_ref[pl.ds(start, wide), :]
        )
    spread_ref[...] = jnp.broadcast_to(factors.astype(jnp.bfloat16)[None], spread_ref.shape)


def widen_call(place, halved, widen, widen_other, token_gain, proj, members):
    rows, channels = halved.shape
    wide = widen.shape[1]
    fine = jax.ShapeDtypeStruct((rows, wide), jnp.bfloat16)
    spread = jax.ShapeDtypeStruct((members, rows // POOL, 2 * PC), jnp.bfloat16)
    return pl.pallas_call(
        widen_kernel,
        out_shape=(fine, fine, spread),
        in_specs=[SMEM] + [VMEM] * 5,
        out_specs=(VMEM,) * 3,
        compiler_params=pltpu.CompilerParams(vmem_limit_bytes=LIMIT),
        cost_estimate=pl.CostEstimate(
            flops=4 * rows * channels * wide,
            bytes_accessed=4 << 20,
            transcendentals=2 * rows * wide,
        ),
        name="widen",
    )(place, halved, widen, widen_other, token_gain, proj)


def arrange_kernel(place_ref, one_ref, other_ref, two_ref, _, out_one_ref, out_two_ref):
    core = place_ref[0]
    part = one_ref.shape[2]
    for a in range(3):
        for b in range(3):
            columns = slice(b * PC, (b + 1) * PC)
            for ref, which in ((one_ref, core), (other_ref, 1 - core)):
                start = pl.multiple_of(a * PC + which * part, part)
                out_one_ref[pl.ds(start, part), columns] = ref[a, b]
            two = two_ref[a, b]
            out_two_ref[a * PC : a * PC + part, columns] = two
            out_two_ref[a * PC + part : (a + 1) * PC, columns] = two


def arrange_call(place, one, other, two, after):
    out = jax.ShapeDtypeStruct((3 * PC, 3 * PC), jnp.bfloat16)
    return pl.pallas_call(
        arrange_kernel,
        out_shape=(out, out),
        in_specs=[SMEM] + [VMEM] * 3 + [ANY],
        out_specs=(VMEM, VMEM),
        compiler_params=pltpu.CompilerParams(vmem_limit_bytes=LIMIT),
        cost_estimate=pl.CostEstimate(flops=0, bytes_accessed=2 << 20, transcendentals=0),
        name="arrange",
    )(place, one, other, two, after)


def pair_kernel(
    tokens_total,
    height,
    width,
    place_ref,
    every_ref,
    dist_ref,
    weight_one_ref,
    weight_two_ref,
    fine_ref,
    fine_received_ref,
    fine_hbm,
    out_hbm,
    row_ref,
    col_ref,
    out_ref,
    sems,
):
    core, row_anchor, col_anchor = place_ref[0], place_ref[2], place_ref[3]
    fine_rows = fine_ref.shape[0]
    copies = []
    for n, (source, which) in enumerate(((fine_ref, core), (fine_received_ref, 1 - core))):
        start = pl.multiple_of(which * fine_rows, fine_rows)
        copies.append(
            pltpu.make_async_copy(source, fine_hbm.at[pl.ds(start, fine_rows)], sems.at[n])
        )
    for copy in copies:
        copy.start()
    per = every_ref.shape[1]
    members = tokens_total // per
    group_start = place_ref[4]
    cols = width + SUB
    high = height + 4
    for ref in (row_ref, col_ref):
        ref[0:SUB] = jnp.zeros((SUB, PC), jnp.float32)
        ref[tokens_total : tokens_total + 2 * SUB] = jnp.zeros((2 * SUB, PC), jnp.float32)
    for m in range(members):
        factors = every_ref[group_start + m].astype(jnp.float32)
        row_ref[2 + m * per : 2 + (m + 1) * per] = factors[:, :PC]
        col_ref[2 + m * per : 2 + (m + 1) * per] = factors[:, PC:]
    col_factor = col_ref[pl.ds(pl.multiple_of(col_anchor, SUB), cols), :]
    j = col_anchor - 2 + iota((cols, PC), 0)
    starts, masks = [], []
    for r in range(high):
        i = row_anchor - 2 + r
        row_factor = row_ref[pl.ds(row_anchor + r, SUB, stride=0), :]
        row_factor = jnp.concatenate([row_factor] * (cols // SUB), axis=0)
        distance = jnp.log1p(jnp.abs(i - j).astype(jnp.float32)) * (1.0 / math.log(tokens_total))
        starts.append(row_factor * col_factor + distance * dist_ref[...])
        masks.append(
            jnp.where((i >= 0) & (i < tokens_total) & (j >= 0) & (j < tokens_total), 1.0, 0.0)
        )
    start = jnp.concatenate(starts, axis=0).astype(jnp.bfloat16).astype(jnp.float32)
    mask = jnp.concatenate(masks, axis=0)

    def conv(active, weight):
        size = active.shape[0]
        shifted = [active] + [pltpu.roll(active, size - b, 0) for b in (1, 2)]
        wide = jnp.concatenate([s.astype(jnp.bfloat16) for s in shifted], axis=1)
        taps = lax.dot_general(
            wide, weight, (((1,), (1,)), ((), ())), preferred_element_type=jnp.float32
        )
        keep = size - 2 * cols
        return sum(taps[a * cols : a * cols + keep, a * PC : (a + 1) * PC] for a in range(3))

    size = high * cols
    centre = pltpu.roll(start, size - 1, 0)[cols : size - cols]
    centre_mask = pltpu.roll(mask, size - 1, 0)[cols : size - cols]
    mid = centre + conv(jax.nn.gelu(start) * mask, weight_one_ref[...])
    mid = mid.astype(jnp.bfloat16).astype(jnp.float32)
    result = conv(jax.nn.gelu(mid) * centre_mask, weight_two_ref[...])
    mid_size = mid.shape[0]
    mid_centre = pltpu.roll(mid, mid_size - 1, 0)[cols : mid_size - cols]
    own = pltpu.roll(mid_centre, core * (PC // 2), 1)
    result = result + own
    channels = out_ref.shape[2]
    for r in range(height):
        out_ref[r] = result[r * cols : r * cols + width, :channels].astype(jnp.bfloat16)
    copies.append(pltpu.make_async_copy(out_ref, out_hbm, sems.at[2]))
    copies[2].start()
    for copy in copies:
        copy.wait()


def pair_call(
    place,
    every,
    dist_weight,
    weight_one,
    weight_two,
    fine,
    fine_received,
    tokens_total,
    height,
    width,
):
    channels = PC // 2
    rows, wide = fine.shape
    return pl.pallas_call(
        functools.partial(pair_kernel, tokens_total, height, width),
        out_shape=(
            jax.ShapeDtypeStruct((2 * rows, wide), jnp.bfloat16),
            jax.ShapeDtypeStruct((height, width, channels), jnp.bfloat16),
        ),
        in_specs=[SMEM] + [VMEM] * 6,
        out_specs=(HBM, HBM),
        scratch_shapes=[
            pltpu.VMEM((tokens_total + 2 * SUB, PC), jnp.float32),
            pltpu.VMEM((tokens_total + 2 * SUB, PC), jnp.float32),
            pltpu.VMEM((height, width, channels), jnp.bfloat16),
            pltpu.SemaphoreType.DMA((3,)),
        ],
        compiler_params=pltpu.CompilerParams(vmem_limit_bytes=32 << 20),
        name="pair",
    )(place, every, dist_weight, weight_one, weight_two, fine, fine_received)


def per_device(
    base_codes,
    stem_weight,
    conv_gain,
    dilated_conv_weight,
    widen_weight,
    token_gain,
    proj_weight,
    dist_weight,
    pair_weight_one,
    pair_weight_two,
):
    seq_count = lax.axis_size("seq")
    section_count = lax.axis_size("section")
    core_count = lax.axis_size("chan")
    chip_count = seq_count * section_count
    members = chip_count * core_count
    group_count = lax.axis_size("groups")
    core = lax.axis_index("chan")
    chip = lax.axis_index(CHIPS)
    last = core_count - 1

    codes = base_codes.reshape(-1, LANES)
    pairs = []
    for g in range(group_count):
        device = [(g * chip_count + i) * core_count for i in range(chip_count)]
        for low, high in zip(device[:-1], device[1:]):
            pairs += [(low + last, high), (high, low + last)]
        following = (g + 1) % group_count * members
        pairs += [(device[0], following), (device[-1] + last, following + members - 1)]
    received = lax.ppermute(codes, ALL, pairs)
    dilated_other = swap(dilated_conv_weight)
    widen_other = swap(widen_weight)
    pair_one = pair_weight_one.swapaxes(2, 3)
    pair_two = pair_weight_two.swapaxes(2, 3)
    pair_one_other = swap(pair_one)

    tokens_total = codes.shape[0] * LANES // PATCH // 2 // POOL * chip_count
    height = tokens_total // seq_count
    width = tokens_total // section_count
    place = jnp.stack(
        [
            core,
            jnp.where(core == 0, chip > 0, chip < chip_count - 1).astype(jnp.int32),
            lax.axis_index("seq") * height,
            lax.axis_index("section") * width,
            lax.axis_index("groups") * members,
        ]
    )
    gain_rows = conv_gain.reshape(-1, LANES)
    token_gain_rows = token_gain.reshape(-1, LANES)
    in_hbm = functools.partial(pltpu.with_memory_space_constraint, memory_space=pltpu.HBM)
    stem, normed, taps, edge_weight, stem_weight, gain_rows, widen_own, token_gain_rows, proj = (
        stem_call(
            place,
            in_hbm(codes),
            in_hbm(stem_weight),
            in_hbm(gain_rows),
            in_hbm(dilated_conv_weight),
            in_hbm(widen_weight),
            in_hbm(token_gain_rows),
            in_hbm(proj_weight),
        )
    )
    halved = tower_call(
        place, received, stem, normed, taps, edge_weight, stem_weight, gain_rows, dilated_other
    )
    fine_own, fine_other, spread = widen_call(
        place, halved, widen_own, widen_other, token_gain_rows, proj, group_count * members
    )
    every = lax.all_to_all(spread, ALL, 0, 0, tiled=True)
    fine_received = swap(fine_other)
    weight_one, weight_two = arrange_call(
        place, pair_one, pair_one_other, pair_two, fine_own
    )
    fine_features, pair_map = pair_call(
        place,
        every,
        dist_weight[None],
        weight_one,
        weight_two,
        fine_own,
        fine_received,
        tokens_total,
        height,
        width,
    )
    return (fine_features, pair_map.transpose(2, 0, 1))


def solution(mesh):
    in_specs = (
        P(("groups", "seq", "section")),
        P(),
        P(),
        P(None, None, "chan"),
        P(None, "chan"),
        P(),
        P(),
        P(),
        P(None, None, None, "chan"),
        P(None, None, None, "chan"),
    )
    out_specs = (P(("groups", "seq", "section"), "chan"), P("chan", ("groups", "seq"), "section"))

    return jax.shard_map(
        per_device, mesh=mesh, in_specs=in_specs, out_specs=out_specs, check_vma=False
    )
```

profile of v0, /device:TPU:0, one launch (start us, length us, event | category | flops | bytes accessed | tf_op | source)
XLA Modules:
  0.0 25.7 jit_solution(17113266393171036254)
XLA Ops:
  0.6 0.6 %collective-permute-start.1 = (bf16[3,768,384]{2,1,0:T(8,128)(2,1)}, bf16[3,768,384]{2,1,0:T(8,128)(2,1)S(1)}, u32[]{:S(2)}, u32[]{:S(2)}) collective-permute-start(bf16[3,768,384]{2,1,0:T(8,128)(2,1)} %dilated_hbm.1), channel_id=1, source_target_pairs={{0,1},{1,0},{2,3},{3,2},{4,5},{5,4},{6,7},{7,6},{8,9},{9,8},{10,11... | collective-permute-start | bytes 5308424 | tf_op jit(solution)/shard_map/ppermute | solution.py:32
  1.2 0.1 collective-permute-start.2
  1.3 2.9 %collective-permute-start = (s32[64,128]{1,0:T(8,128)}, s32[64,128]{1,0:T(8,128)S(1)}, u32[]{:S(2)}, u32[]{:S(2)}) collective-permute-start(s32[64,128]{1,0:T(8,128)} %bitcast.16), channel_id=1, source_target_pairs={{1,2},{2,1},{3,4},{4,3},{5,6},{6,5},{7,8},{8,7},{9,10},{10,9},{11,... | collective-permute-start | bytes 98312 | tf_op jit(solution)/shard_map/ppermute | solution.py:492
  4.2 0.1 stack.27.place_ref
  4.3 3.1 %stem.1 = (bf16[256,768]{1,0:T(8,128)(2,1)S(1)}, bf16[272,768]{1,0:T(8,128)(2,1)S(1)}, f32[256,384]{1,0:T(8,128)S(1)}, bf16[768,384]{1,0:T(8,128)(2,1)S(1)}, bf1...) custom-call(s32[5]{0:T(128)S(1)} %stack.27.place_ref, ...), custom_call_target="tpu_custom_call" | custom-call | flops 452984832 | bytes 4194304 | tf_op jit(solution)/shard_map/stem/pallas_call | solution.py:157
  7.4 0.0 collective-permute-done.received_ref
  7.4 0.0 collective-permute-done.1.dilated_ref
  7.4 1.8 %tower.1.halved_ref = bf16[128,768]{1,0:T(8,128)(2,1)S(1)} custom-call(s32[5]{0:T(128)S(1)} %stack.27.place_ref, s32[64,128]{1,0:T(8,128)S(1)} %collective-permute-done.received_ref, bf16[256,768]{1,0:T(8,128)(2,1)S(1)} %get-tuple-element.18.stem_ref, bf16[272,768]{1,0:T(8,128)(2,1)S(1)} %get-tuple-element.19.normed_ref, ...), custom_call_target="tpu_custom_call" | custom-call | flops 452984832 | bytes 4194304 | tf_op jit(solution)/shard_map/tower/pallas_call | solution.py:232
  9.2 0.0 collective-permute-done.2.widen_other_ref
  9.2 0.0 copy-start
  9.2 0.0 copy-start.1
  9.3 0.0 copy-start.2
  9.3 2.1 %widen.1 = (bf16[128,768]{1,0:T(8,128)(2,1)S(1)}, bf16[128,768]{1,0:T(8,128)(2,1)S(1)}, bf16[32,2,256]{2,1,0:T(2,128)(2,1)}) custom-call(s32[5]{0:T(128)S(1)} %stack.27.place_ref, bf16[128,768]{1,0:T(8,128)(2,1)S(1)} %tower.1.halved_ref, bf16[768,768]{1,0:T(8,128)(2,1)S(1)} %get-tuple-element.24.widen_ref, ...), custom_call_target="tpu_custom_call" | custom-call | flops 301989888 | bytes 4194304 | tf_op jit(solution)/shard_map/widen/pallas_call | solution.py:303
  11.4 0.1 collective-permute-start.4
  11.5 0.0 copy-done
  11.5 0.4 %collective-permute-start.3 = (bf16[3,3,64,128]{3,2,1,0:T(8,128)(2,1)S(1)}, bf16[3,3,64,128]{3,2,1,0:T(8,128)(2,1)S(1)}, u32[]{:S(2)}, u32[]{:S(2)}) collective-permute-start(bf16[3,3,64,128]{3,2,1,0:T(8,128)(2,1)S(1)} %bitcast.12), channel_id=1, source_target_pairs={{0,1},{1,0},{2,3},{3,2},{4,5},{5,4},{6,7},{7,6},{8,9},{9,8},{10,11... | collective-permute-start | bytes 442376 | tf_op jit(solution)/shard_map/ppermute | solution.py:32
  11.9 4.7 %all-to-all-start = ((bf16[32,2,256]{2,1,0:T(2,128)(2,1)}), bf16[32,2,256]{2,1,0:T(2,128)(2,1)S(1)}, u32[]{:S(2)}, u32[]{:S(2)}) async-start(bf16[32,2,256]{2,1,0:T(2,128)(2,1)} %get-tuple-element.27), calls=%async_computation | async-start | bytes 65536 | tf_op jit(solution)/shard_map/all_to_all | solution.py:532
  16.6 0.0 collective-permute-done.3.other_ref
  16.6 0.0 copy-done.1
  16.6 0.6 %arrange.1 = (bf16[384,384]{1,0:T(8,128)(2,1)S(1)}, bf16[384,384]{1,0:T(8,128)(2,1)S(1)}) custom-call(s32[5]{0:T(128)S(1)} %stack.27.place_ref, bf16[3,3,64,128]{3,2,1,0:T(8,128)(2,1)S(1)} %bitcast.13, bf16[3,3,64,128]{3,2,1,0:T(8,128)(2,1)S(1)} %collective-permute-done.3.other_ref, bf16[3,3,64,128]{3,2,1,0:T(8,128)(2,1)S(1)} %bitcast.14, ...), custom_call_target="tpu_custom_call" | custom-call | bytes 2097152 | tf_op jit(solution)/shard_map/arrange/pallas_call | solution.py:334
  17.3 6.6 %all-to-all-done.every_ref = bf16[32,2,256]{2,1,0:T(2,128)(2,1)S(1)} async-done(((bf16[32,2,256]{2,1,0:T(2,128)(2,1)}), bf16[32,2,256]{2,1,0:T(2,128)(2,1)S(1)}, u32[]{:S(2)}, u32[]{:S(2)}) %all-to-all-start) | async-done | bytes 32800 | tf_op jit(solution)/shard_map/all_to_all | solution.py:532
  23.9 0.0 collective-permute-done.4.fine_received_ref
  23.9 0.0 copy-done.2
  23.9 1.9 %pair.1 = (bf16[256,768]{1,0:T(8,128)(2,1)}, bf16[8,16,64]{2,1,0:T(8,128)(2,1)}) custom-call(s32[5]{0:T(128)S(1)} %stack.27.place_ref, bf16[32,2,256]{2,1,0:T(2,128)(2,1)S(1)} %all-to-all-done.every_ref, f32[1,128]{1,0:T(1,128)S(1)} %bitcast.15, bf16[384,384]{1,0:T(8,128)(2,1)S(1)} %get-tuple-element.29.weight_one_ref, ...), custom_call_target="tpu_custom_call" | custom-call | tf_op jit(solution)/shard_map/pair/pallas_call | solution.py:443
Async XLA Ops:
  0.6 6.7 %collective-permute-start.1 = (bf16[3,768,384]{2,1,0:T(8,128)(2,1)}, bf16[3,768,384]{2,1,0:T(8,128)(2,1)S(1)}, u32[]{:S(2)}, u32[]{:S(2)}) collective-permute-start(bf16[3,768,384]{2,1,0:T(8,128)(2,1)} %dilated_hbm.1), channel_id=1, source_target_pairs={{0,1},{1,0},{2,3},{3,2},{4,5},{5,4},{6,7},{7,6},{8,9},{9,8},{10,11... | collective-permute-start | bytes 5308424 | tf_op jit(solution)/shard_map/ppermute | solution.py:32
  1.2 8.0 %collective-permute-start.2 = (bf16[768,768]{1,0:T(8,128)(2,1)}, bf16[768,768]{1,0:T(8,128)(2,1)S(1)}, u32[]{:S(2)}, u32[]{:S(2)}) collective-permute-start(bf16[768,768]{1,0:T(8,128)(2,1)} %widen_hbm.1), channel_id=1, source_target_pairs={{0,1},{1,0},{2,3},{3,2},{4,5},{5,4},{6,7},{7,6},{8,9},{9,8},{10,11... | collective-permute-start | bytes 3538952 | tf_op jit(solution)/shard_map/ppermute | solution.py:32
  1.3 6.1 %collective-permute-start = (s32[64,128]{1,0:T(8,128)}, s32[64,128]{1,0:T(8,128)S(1)}, u32[]{:S(2)}, u32[]{:S(2)}) collective-permute-start(s32[64,128]{1,0:T(8,128)} %bitcast.16), channel_id=1, source_target_pairs={{1,2},{2,1},{3,4},{4,3},{5,6},{6,5},{7,8},{8,7},{9,10},{10,9},{11,... | collective-permute-start | bytes 98312 | tf_op jit(solution)/shard_map/ppermute | solution.py:492
  9.2 2.2 %copy-start = (bf16[3,3,128,64]{2,3,1,0:T(8,128)(2,1)S(1)}, bf16[3,3,128,64]{2,3,1,0:T(8,128)(2,1)}, u32[]{:S(2)}) copy-start(bf16[3,3,128,64]{2,3,1,0:T(8,128)(2,1)} %param.18) | copy-start | bytes 442372
  9.2 7.4 %copy-start.1 = (bf16[3,3,128,64]{2,3,1,0:T(8,128)(2,1)S(1)}, bf16[3,3,128,64]{2,3,1,0:T(8,128)(2,1)}, u32[]{:S(2)}) copy-start(bf16[3,3,128,64]{2,3,1,0:T(8,128)(2,1)} %param.19) | copy-start | bytes 442372
  9.3 14.6 %copy-start.2 = (f32[128]{0:T(128)S(1)}, f32[128]{0:T(128)}, u32[]{:S(2)}) copy-start(f32[128]{0:T(128)} %param.17) | copy-start | bytes 1540
  11.4 12.5 %collective-permute-start.4 = (bf16[128,768]{1,0:T(8,128)(2,1)S(1)}, bf16[128,768]{1,0:T(8,128)(2,1)S(1)}, u32[]{:S(2)}, u32[]{:S(2)}) collective-permute-start(bf16[128,768]{1,0:T(8,128)(2,1)S(1)} %get-tuple-element.31), channel_id=1, source_target_pairs={{0,1},{1,0},{2,3},{3,2},{4,5},{5,4},{6,7},{7,6},{8,9},{9,8},{10,11... | collective-permute-start | bytes 589832 | tf_op jit(solution)/shard_map/ppermute | solution.py:32
  11.5 5.1 %collective-permute-start.3 = (bf16[3,3,64,128]{3,2,1,0:T(8,128)(2,1)S(1)}, bf16[3,3,64,128]{3,2,1,0:T(8,128)(2,1)S(1)}, u32[]{:S(2)}, u32[]{:S(2)}) collective-permute-start(bf16[3,3,64,128]{3,2,1,0:T(8,128)(2,1)S(1)} %bitcast.12), channel_id=1, source_target_pairs={{0,1},{1,0},{2,3},{3,2},{4,5},{5,4},{6,7},{7,6},{8,9},{9,8},{10,11... | collective-permute-start | bytes 442376 | tf_op jit(solution)/shard_map/ppermute | solution.py:32
  11.9 12.0 %all-to-all-start = ((bf16[32,2,256]{2,1,0:T(2,128)(2,1)}), bf16[32,2,256]{2,1,0:T(2,128)(2,1)S(1)}, u32[]{:S(2)}, u32[]{:S(2)}) async-start(bf16[32,2,256]{2,1,0:T(2,128)(2,1)} %get-tuple-element.27), calls=%async_computation | async-start | bytes 65536 | tf_op jit(solution)/shard_map/all_to_all | solution.py:532
where the time goes:
time: 25.9 us; the launch traced here: 25.7 us
  Pallas kernels  9.52 us (37%)
  starting transfers between devices  8.78 us (34%)
  waiting for transfers between devices  6.61 us (26%)
  between operations  0.73 us (3%)
    all_to_all x1, waiting for transfers between devices, per_device(): every = lax.all_to_all(spread, ALL, 0, 0, tiled=True)  6.59 us
    all_to_all x1, starting transfers between devices, per_device(): every = lax.all_to_all(spread, ALL, 0, 0, tiled=True)  4.7 us
    pallas_call x1, Pallas kernels, stem_call(): pl.pallas_call(stem_kernel, out_shape=out_shape, in_specs=[SMEM] + [HBM]...  3.06 us
    ppermute x1, starting transfers between devices, per_device(): received = lax.ppermute(codes, ALL, pairs)  2.93 us
    pallas_call x1, Pallas kernels, widen_call(): pl.pallas_call(widen_kernel, out_shape=(fine, fine, spread), in_specs=[SM...  2.12 us
    pallas_call x1, Pallas kernels, pair_call(): pl.pallas_call(functools.partial(pair_kernel, tokens_total, height, width...  1.86 us
    pallas_call x1, Pallas kernels, tower_call(): pl.pallas_call(tower_kernel, out_shape=jax.ShapeDtypeStruct((rows // 2, c...  1.84 us
    ppermute x4, starting transfers between devices, swap(): lax.ppermute(values, 'chan', [(i, count - 1 - i) for i in range(count)])  1.15 us
  transfers between devices with their start and end apart: 6, of which 1 were waited for; matrix products, arithmetic and copies ran while one was open for 0% of the time, Pallas kernels for 22%

commit v1 on v0

--- a/solution.py
+++ b/solution.py
@@ -36,6 +36,16 @@
     return jnp.dot(a, b, preferred_element_type=jnp.float32)
 
 
+def gelu_of(part, share):
+    linear = math.sqrt(2 / math.pi) / share
+    cubic = 0.044715 * math.sqrt(2 / math.pi) / share**3
+    return part + part * jnp.tanh(part * (linear + cubic * (part * part)))
+
+
+def gelu(x):
+    return gelu_of(0.5 * x, 0.5)
+
+
 def iota(shape, axis):
     return lax.broadcasted_iota(jnp.int32, shape, axis)
 
@@ -52,23 +62,23 @@
 
 def stem_of(codes, valid, stem_weight, gain):
     base = (iota(codes.shape, 1) % 4).astype(jnp.float32)
-    onehot = jnp.where((codes == base) & valid, 1.0, 0.0).astype(jnp.bfloat16)
-    stem = dot(onehot, stem_weight).astype(jnp.bfloat16).astype(jnp.float32)
+    onehot = jnp.where((codes == base) & valid, 0.5, 0.0).astype(jnp.bfloat16)
+    stem = dot(onehot, stem_weight)
     mean_square = jnp.mean(stem * stem, axis=1, keepdims=True)
-    normed = (stem * lax.rsqrt(mean_square + epsilon) * gain).astype(jnp.bfloat16)
-    return stem, normed
+    scale = 0.25 * lax.rsqrt(mean_square + 0.25 * epsilon)
+    return stem, (stem * scale * gain).astype(jnp.bfloat16)
 
 
 def in_lanes(rows):
     return jnp.concatenate([rows[r : r + 1] for r in range(rows.shape[0])], axis=1)
 
 
-def taps_of(normed, weight_ref, sum_ref, rows):
-    first = dot(normed, weight_ref[0])
-    centre = dot(normed, weight_ref[1])
-    third = dot(normed, weight_ref[2])
-    sum_ref[...] = first[: rows + SUB] + third[SUB:]
-    return centre[SUB : SUB + rows] + sum_ref[DILATION_ROWS : DILATION_ROWS + rows]
+def taps_of(normed, weight_ref, sum_ref, rows, columns):
+    first = dot(normed, weight_ref[0, :, columns])
+    third = dot(normed, weight_ref[2, :, columns])
+    centre = dot(normed, weight_ref[1, :, columns])
+    sum_ref[:, columns] = first[: rows + SUB] + third[SUB:]
+    return centre[SUB : SUB + rows] + sum_ref[DILATION_ROWS : DILATION_ROWS + rows, columns]
 
 
 def stem_kernel(
@@ -80,6 +90,8 @@
     widen_hbm,
     token_gain_hbm,
     proj_hbm,
+    pair_one_hbm,
+    pair_two_hbm,
     stem_ref,
     normed_ref,
     taps_ref,
@@ -89,6 +101,8 @@
     widen_ref,
     token_gain_ref,
     proj_ref,
+    pair_one_ref,
+    pair_two_ref,
     codes_ref,
     near_ref,
     dilated_ref,
@@ -106,6 +120,8 @@
                 (widen_hbm, widen_ref),
                 (token_gain_hbm, token_gain_ref),
                 (proj_hbm, proj_ref),
+                (pair_one_hbm, pair_one_ref),
+                (pair_two_hbm, pair_two_ref),
             )
         )
     ]
@@ -132,13 +148,13 @@
     stem_ref[...] = stem[SUB : SUB + rows].astype(jnp.bfloat16)
     normed_ref[...] = normed
     copies[3].wait()
-    taps_ref[...] = taps_of(normed, dilated_ref, sum_ref, rows)
+    taps_ref[...] = taps_of(normed, dilated_ref, sum_ref, rows, slice(0, dilated_ref.shape[2]))
     edge_weight_ref[...] = dilated_ref[2 * core]
     for copy in copies[4:]:
         copy.wait()
 
 
-def stem_call(place, codes, stem_weight, conv_gain, dilated, widen, token_gain, proj):
+def stem_call(place, codes, stem_weight, conv_gain, dilated, widen, token_gain, proj, one, two):
     channels = stem_weight.shape[1]
     half = dilated.shape[2]
     rows = codes.shape[0] // 2 * SUB
@@ -153,25 +169,27 @@
         shape(widen.shape, jnp.bfloat16),
         shape(token_gain.shape, jnp.float32),
         shape(proj.shape, jnp.bfloat16),
+        shape(one.shape, jnp.bfloat16),
+        shape(two.shape, jnp.bfloat16),
     )
     return pl.pallas_call(
         stem_kernel,
         out_shape=out_shape,
-        in_specs=[SMEM] + [HBM] * 7,
+        in_specs=[SMEM] + [HBM] * 9,
         out_specs=(VMEM,) * len(out_shape),
         scratch_shapes=[
             pltpu.VMEM(codes.shape, jnp.int32),
             pltpu.VMEM((codes.shape[0] // 2 + 3 * SUB, LANES), jnp.int32),
             pltpu.VMEM(dilated.shape, jnp.bfloat16),
             pltpu.VMEM((rows + SUB, half), jnp.float32),
-            pltpu.SemaphoreType.DMA((7,)),
+            pltpu.SemaphoreType.DMA((9,)),
         ],
         compiler_params=pltpu.CompilerParams(vmem_limit_bytes=LIMIT),
         cost_estimate=pl.CostEstimate(
             flops=6 * rows * channels * half, bytes_accessed=4 << 20, transcendentals=0
         ),
         name="stem",
-    )(place, codes, stem_weight, conv_gain, dilated, widen, token_gain, proj)
+    )(place, codes, stem_weight, conv_gain, dilated, widen, token_gain, proj, one, two)
 
 
 def tower_kernel(
@@ -191,7 +209,6 @@
 ):
     core, outside = place_ref[0], place_ref[1]
     rows = stem_ref.shape[0]
-    half = taps_ref.shape[1]
     end = received_ref.shape[0]
     near_ref[0:SUB] = jnp.where(core == 0, received_ref[end - SUB :], received_ref[:SUB])
     near_ref[SUB:] = jnp.zeros((SUB, LANES), jnp.int32)
@@ -200,30 +217,37 @@
         near_ref[pl.ds(SUB - 1, SUB, stride=0), :],
         near_ref[pl.ds(0, SUB, stride=0), :],
     )
+    normed = normed_ref[...]
+    width = taps_ref.shape[1]
+    chunks = [slice(0, width)]
     _, edge = stem_of(
         spread_codes([tile]), outside > 0, stem_weight_ref[...], in_lanes(conv_gain_ref[...])
     )
-    other_taps = taps_of(normed_ref[...], dilated_ref, sum_ref, rows)
-    for taps, edge_weight, which in (
-        (taps_ref[...], edge_weight_ref[...], core),
-        (other_taps, dilated_ref[2 * core], 1 - core),
-    ):
-        added = pltpu.roll(dot(edge, edge_weight), DILATION_ROWS, 0)
+
+    parts = [taps_of(normed, dilated_ref, sum_ref, rows, chunk) for chunk in chunks]
+
+    def finish(taps, added, which, first_column, slot):
+        added = pltpu.roll(added, DILATION_ROWS, 0)
         row = iota(added.shape, 0)
         head = jnp.where((row < DILATION_ROWS) & (core == 0), added, 0.0)
         tail = jnp.where((row >= DILATION_ROWS) & (core > 0), added, 0.0)
         taps = jnp.concatenate(
             [taps[:SUB] + head, taps[SUB : rows - SUB], taps[rows - SUB :] + tail], axis=0
         )
-        columns = pl.ds(pl.multiple_of(which * half, LANES), half)
-        tower = stem_ref[:, columns].astype(jnp.float32) + jax.nn.gelu(taps)
-        pooled = []
-        for c in range(half // LANES):
-            tower_ref[c] = tower[:, c * LANES : (c + 1) * LANES]
-            even = tower_ref[c, pl.ds(0, rows // 2, stride=2), :]
-            odd = tower_ref[c, pl.ds(1, rows // 2, stride=2), :]
-            pooled.append(jnp.maximum(even, odd))
-        halved_ref[:, columns] = jnp.concatenate(pooled, axis=1).astype(jnp.bfloat16)
+        for c in range(0, taps.shape[1], LANES):
+            start = pl.multiple_of(which * width + first_column + c, LANES)
+            columns = pl.ds(start, LANES)
+            stem = stem_ref[:, columns].astype(jnp.float32)
+            slot_ref = tower_ref.at[slot + c // LANES]
+            slot_ref[...] = stem + gelu_of(taps[:, c : c + LANES], 0.25)
+            even = slot_ref[pl.ds(0, rows // 2, stride=2), :]
+            odd = slot_ref[pl.ds(1, rows // 2, stride=2), :]
+            halved_ref[:, columns] = jnp.maximum(even, odd).astype(jnp.bfloat16)
+
+    finish(taps_ref[...], dot(edge, edge_weight_ref[...]), core, 0, 0)
+    for part, chunk in zip(parts, chunks):
+        added = dot(edge, dilated_ref[2 * core, :, chunk])
+        finish(part, added, 1 - core, chunk.start, (width + chunk.start) // LANES)
 
 
 def tower_call(place, received, stem, normed, taps, edge_weight, stem_weight, conv_gain, dilated):
@@ -237,7 +261,7 @@
         scratch_shapes=[
             pltpu.VMEM((2 * SUB, LANES), jnp.int32),
             pltpu.VMEM((rows + SUB, half), jnp.float32),
-            pltpu.VMEM((half // LANES, rows, LANES), jnp.float32),
+            pltpu.VMEM((channels // LANES, rows, LANES), jnp.float32),
         ],
         compiler_params=pltpu.CompilerParams(vmem_limit_bytes=LIMIT),
         cost_estimate=pl.CostEstimate(
@@ -263,35 +287,36 @@
     core = place_ref[0]
     halved = halved_ref[...]
     token_count = halved.shape[0] // POOL
-    tokens = []
-    for weight_ref, out_ref in ((widen_ref, fine_ref), (widen_other_ref, fine_other_ref)):
-        fine = jax.nn.gelu(dot(halved, weight_ref[...])).astype(jnp.bfloat16)
-        out_ref[...] = fine
-        fine = fine.astype(jnp.float32)
-        tokens.append(
-            jnp.concatenate(
-                [
-                    jnp.mean(fine[t * POOL : (t + 1) * POOL], axis=0, keepdims=True)
-                    for t in range(token_count)
-                ],
-                axis=0,
-            )
-            .astype(jnp.bfloat16)
-            .astype(jnp.float32)
-        )
     wide = widen_ref.shape[1]
-    squares = sum(jnp.sum(t * t, axis=1, keepdims=True) for t in tokens)
-    scale = lax.rsqrt(squares / (2 * wide) + epsilon)
     gain = token_gain_ref[...]
     gain_rows = wide // LANES
     gains = [in_lanes(gain[:gain_rows]), in_lanes(gain[gain_rows:])]
-    factors = 0.0
-    for token, which in zip(tokens, (core, 1 - core)):
+    squares, factors = 0.0, 0.0
+    for weight_ref, out_ref, which in (
+        (widen_ref, fine_ref, core),
+        (widen_other_ref, fine_other_ref, 1 - core),
+    ):
+        pieces = []
+        for c in range(0, wide, 2 * LANES):
+            columns = slice(c, c + 2 * LANES)
+            fine = gelu_of(dot(halved, weight_ref[:, columns]), 0.5)
+            out_ref[:, columns] = fine.astype(jnp.bfloat16)
+            pieces.append(
+                jnp.concatenate(
+                    [
+                        jnp.sum(fine[t * POOL : (t + 1) * POOL], axis=0, keepdims=True)
+                        for t in range(token_count)
+                    ],
+                    axis=0,
+                )
+            )
+        token = jnp.concatenate(pieces, axis=1) * (1.0 / POOL)
+        token = token.astype(jnp.bfloat16).astype(jnp.float32)
+        squares = squares + jnp.sum(token * token, axis=1, keepdims=True)
         start = pl.multiple_of(which * wide, LANES)
-        gain = jnp.where(which == 0, gains[0], gains[1])
-        factors = factors + dot(
-            (token * scale * gain).astype(jnp.bfloat16), proj_ref[pl.ds(start, wide), :]
-        )
+        scaled = (token * jnp.where(which == 0, gains[0], gains[1])).astype(jnp.bfloat16)
+        factors = factors + dot(scaled, proj_ref[pl.ds(start, wide), :])
+    factors = factors * lax.rsqrt(squares / (2 * wide) + epsilon)
     spread_ref[...] = jnp.broadcast_to(factors.astype(jnp.bfloat16)[None], spread_ref.shape)
 
 
@@ -315,33 +340,6 @@
     )(place, halved, widen, widen_other, token_gain, proj)
 
 
-def arrange_kernel(place_ref, one_ref, other_ref, two_ref, _, out_one_ref, out_two_ref):
-    core = place_ref[0]
-    part = one_ref.shape[2]
-    for a in range(3):
-        for b in range(3):
-            columns = slice(b * PC, (b + 1) * PC)
-            for ref, which in ((one_ref, core), (other_ref, 1 - core)):
-                start = pl.multiple_of(a * PC + which * part, part)
-                out_one_ref[pl.ds(start, part), columns] = ref[a, b]
-            two = two_ref[a, b]
-            out_two_ref[a * PC : a * PC + part, columns] = two
-            out_two_ref[a * PC + part : (a + 1) * PC, columns] = two
-
-
-def arrange_call(place, one, other, two, after):
-    out = jax.ShapeDtypeStruct((3 * PC, 3 * PC), jnp.bfloat16)
-    return pl.pallas_call(
-        arrange_kernel,
-        out_shape=(out, out),
-        in_specs=[SMEM] + [VMEM] * 3 + [ANY],
-        out_specs=(VMEM, VMEM),
-        compiler_params=pltpu.CompilerParams(vmem_limit_bytes=LIMIT),
-        cost_estimate=pl.CostEstimate(flops=0, bytes_accessed=2 << 20, transcendentals=0),
-        name="arrange",
-    )(place, one, other, two, after)
-
-
 def pair_kernel(
     tokens_total,
     height,
@@ -350,6 +348,7 @@
     every_ref,
     dist_ref,
     weight_one_ref,
+    weight_other_ref,
     weight_two_ref,
     fine_ref,
     fine_received_ref,
@@ -397,7 +396,13 @@
     start = jnp.concatenate(starts, axis=0).astype(jnp.bfloat16).astype(jnp.float32)
     mask = jnp.concatenate(masks, axis=0)
 
-    def conv(active, weight):
+    def across(ref, a):
+        return jnp.concatenate([ref[a, b] for b in range(3)], axis=1)
+
+    def conv(active, first_ref, second_ref):
+        weight = jnp.concatenate(
+            [across(ref, a) for a in range(3) for ref in (first_ref, second_ref)], axis=0
+        )
         size = active.shape[0]
         shifted = [active] + [pltpu.roll(active, size - b, 0) for b in (1, 2)]
         wide = jnp.concatenate([s.astype(jnp.bfloat16) for s in shifted], axis=1)
@@ -410,9 +415,10 @@
     size = high * cols
     centre = pltpu.roll(start, size - 1, 0)[cols : size - cols]
     centre_mask = pltpu.roll(mask, size - 1, 0)[cols : size - cols]
-    mid = centre + conv(jax.nn.gelu(start) * mask, weight_one_ref[...])
+    added = conv(gelu(start) * mask, weight_one_ref, weight_other_ref)
+    mid = centre + pltpu.roll(added, core * (PC // 2), 1)
     mid = mid.astype(jnp.bfloat16).astype(jnp.float32)
-    result = conv(jax.nn.gelu(mid) * centre_mask, weight_two_ref[...])
+    result = conv(gelu(mid) * centre_mask, weight_two_ref, weight_two_ref)
     mid_size = mid.shape[0]
     mid_centre = pltpu.roll(mid, mid_size - 1, 0)[cols : mid_size - cols]
     own = pltpu.roll(mid_centre, core * (PC // 2), 1)
@@ -431,6 +437,7 @@
     every,
     dist_weight,
     weight_one,
+    weight_other,
     weight_two,
     fine,
     fine_received,
@@ -446,7 +453,7 @@
             jax.ShapeDtypeStruct((2 * rows, wide), jnp.bfloat16),
             jax.ShapeDtypeStruct((height, width, channels), jnp.bfloat16),
         ),
-        in_specs=[SMEM] + [VMEM] * 6,
+        in_specs=[SMEM] + [VMEM] * 7,
         out_specs=(HBM, HBM),
         scratch_shapes=[
             pltpu.VMEM((tokens_total + 2 * SUB, PC), jnp.float32),
@@ -456,7 +463,7 @@
         ],
         compiler_params=pltpu.CompilerParams(vmem_limit_bytes=32 << 20),
         name="pair",
-    )(place, every, dist_weight, weight_one, weight_two, fine, fine_received)
+    )(place, every, dist_weight, weight_one, weight_other, weight_two, fine, fine_received)
 
 
 def per_device(
@@ -492,6 +499,7 @@
     received = lax.ppermute(codes, ALL, pairs)
     dilated_other = swap(dilated_conv_weight)
     widen_other = swap(widen_weight)
+    in_hbm = functools.partial(pltpu.with_memory_space_constraint, memory_space=pltpu.HBM)
     pair_one = pair_weight_one.swapaxes(2, 3)
     pair_two = pair_weight_two.swapaxes(2, 3)
     pair_one_other = swap(pair_one)
@@ -510,18 +518,29 @@
     )
     gain_rows = conv_gain.reshape(-1, LANES)
     token_gain_rows = token_gain.reshape(-1, LANES)
-    in_hbm = functools.partial(pltpu.with_memory_space_constraint, memory_space=pltpu.HBM)
-    stem, normed, taps, edge_weight, stem_weight, gain_rows, widen_own, token_gain_rows, proj = (
-        stem_call(
-            place,
-            in_hbm(codes),
-            in_hbm(stem_weight),
-            in_hbm(gain_rows),
-            in_hbm(dilated_conv_weight),
-            in_hbm(widen_weight),
-            in_hbm(token_gain_rows),
-            in_hbm(proj_weight),
-        )
+    (
+        stem,
+        normed,
+        taps,
+        edge_weight,
+        stem_weight,
+        gain_rows,
+        widen_own,
+        token_gain_rows,
+        proj,
+        pair_one,
+        pair_two,
+    ) = stem_call(
+        place,
+        in_hbm(codes),
+        in_hbm(stem_weight),
+        in_hbm(gain_rows),
+        in_hbm(dilated_conv_weight),
+        in_hbm(widen_weight),
+        in_hbm(token_gain_rows),
+        in_hbm(proj_weight),
+        in_hbm(pair_one),
+        in_hbm(pair_two),
     )
     halved = tower_call(
         place, received, stem, normed, taps, edge_weight, stem_weight, gain_rows, dilated_other
@@ -529,17 +548,15 @@
     fine_own, fine_other, spread = widen_call(
         place, halved, widen_own, widen_other, token_gain_rows, proj, group_count * members
     )
+    fine_received = swap(fine_other)
     every = lax.all_to_all(spread, ALL, 0, 0, tiled=True)
-    fine_received = swap(fine_other)
-    weight_one, weight_two = arrange_call(
-        place, pair_one, pair_one_other, pair_two, fine_own
-    )
     fine_features, pair_map = pair_call(
         place,
         every,
         dist_weight[None],
-        weight_one,
-        weight_two,
+        pair_one,
+        pair_one_other,
+        pair_two,
         fine_own,
         fine_received,
         tokens_total,

time: 25.9 us -> 25.8 us (level)
  Pallas kernels: 9.52 us -> 8.82 us
  waiting for transfers between devices: 6.61 us -> 7.26 us
    all_to_all x1, waiting for transfers between devices: 6.59 us -> 7.24 us  [per_device(): every = lax.all_to_all(spread, ALL, 0, 0, tiled=True)]
    pallas_call x1 -> x0, Pallas kernels: 0.63 us -> none  [arrange_call(): pl.pallas_call(arrange_kernel, out_shape=(out, out), in_specs=[SMEM] + [V...]
  transfers between devices with their start and end apart: 6 -> 6, of which waited for: 1 -> 1; matrix products, arithmetic and copies ran while one was open for 0% -> 0% of each run, Pallas kernels for 22% -> 19%
where the time goes in v1:
time: 25.8 us; the launch traced here: 25.6 us
  Pallas kernels  8.82 us (34%)
  starting transfers between devices  8.77 us (34%)
  waiting for transfers between devices  7.26 us (28%)
  between operations  0.71 us (3%)
    all_to_all x1, waiting for transfers between devices, per_device(): every = lax.all_to_all(spread, ALL, 0, 0, tiled=True)  7.24 us
    all_to_all x1, starting transfers between devices, per_device(): every = lax.all_to_all(spread, ALL, 0, 0, tiled=True)  4.69 us
    pallas_call x1, Pallas kernels, stem_call(): pl.pallas_call(stem_kernel, out_shape=out_shape, in_specs=[SMEM] + [HBM]...  3.08 us
    ppermute x1, starting transfers between devices, per_device(): received = lax.ppermute(codes, ALL, pairs)  2.93 us
    pallas_call x1, Pallas kernels, widen_call(): pl.pallas_call(widen_kernel, out_shape=(fine, fine, spread), in_specs=[SM...  1.98 us
    pallas_call x1, Pallas kernels, pair_call(): pl.pallas_call(functools.partial(pair_kernel, tokens_total, height, width...  1.94 us
    pallas_call x1, Pallas kernels, tower_call(): pl.pallas_call(tower_kernel, out_shape=jax.ShapeDtypeStruct((rows // 2, c...  1.82 us
    ppermute x4, starting transfers between devices, swap(): lax.ppermute(values, 'chan', [(i, count - 1 - i) for i in range(count)])  1.15 us
  transfers between devices with their start and end apart: 6, of which 1 were waited for; matrix products, arithmetic and copies ran while one was open for 0% of the time, Pallas kernels for 19%

profile of v1, /device:TPU:0, one launch (start us, length us, event | category | flops | bytes accessed | tf_op | source)
XLA Modules:
  0.0 25.6 jit_solution(18043456557705706752)
XLA Ops:
  0.6 0.6 %collective-permute-start.1 = (bf16[3,768,384]{2,1,0:T(8,128)(2,1)}, bf16[3,768,384]{2,1,0:T(8,128)(2,1)S(1)}, u32[]{:S(2)}, u32[]{:S(2)}) collective-permute-start(bf16[3,768,384]{2,1,0:T(8,128)(2,1)} %dilated_hbm.1), channel_id=1, source_target_pairs={{0,1},{1,0},{2,3},{3,2},{4,5},{5,4},{6,7},{7,6},{8,9},{9,8},{10,11... | collective-permute-start | bytes 5308424 | tf_op jit(solution)/shard_map/ppermute | solution.py:32
  1.2 0.1 collective-permute-start.2
  1.3 2.9 %collective-permute-start = (s32[64,128]{1,0:T(8,128)}, s32[64,128]{1,0:T(8,128)S(1)}, u32[]{:S(2)}, u32[]{:S(2)}) collective-permute-start(s32[64,128]{1,0:T(8,128)} %bitcast.16), channel_id=1, source_target_pairs={{1,2},{2,1},{3,4},{4,3},{5,6},{6,5},{7,8},{8,7},{9,10},{10,9},{11,... | collective-permute-start | bytes 98312 | tf_op jit(solution)/shard_map/ppermute | solution.py:499
  4.2 0.1 stack.27.place_ref
  4.3 3.1 %stem.1 = (bf16[256,768]{1,0:T(8,128)(2,1)S(1)}, bf16[272,768]{1,0:T(8,128)(2,1)S(1)}, f32[256,384]{1,0:T(8,128)S(1)}, bf16[768,384]{1,0:T(8,128)(2,1)S(1)}, bf1...) custom-call(s32[5]{0:T(128)S(1)} %stack.27.place_ref, ...), custom_call_target="tpu_custom_call" | custom-call | flops 452984832 | bytes 4194304 | tf_op jit(solution)/shard_map/stem/pallas_call | solution.py:175
  7.4 0.0 collective-permute-done.received_ref
  7.4 0.0 collective-permute-done.1.dilated_ref
  7.4 1.8 %tower.1.halved_ref = bf16[128,768]{1,0:T(8,128)(2,1)S(1)} custom-call(s32[5]{0:T(128)S(1)} %stack.27.place_ref, s32[64,128]{1,0:T(8,128)S(1)} %collective-permute-done.received_ref, bf16[256,768]{1,0:T(8,128)(2,1)S(1)} %get-tuple-element.18.stem_ref, bf16[272,768]{1,0:T(8,128)(2,1)S(1)} %get-tuple-element.19.normed_ref, ...), custom_call_target="tpu_custom_call" | custom-call | flops 452984832 | bytes 4194304 | tf_op jit(solution)/shard_map/tower/pallas_call | solution.py:256
  9.2 0.0 collective-permute-done.2.widen_other_ref
  9.2 0.0 copy-start.1
  9.2 0.0 copy-start
  9.3 2.0 %widen.1 = (bf16[128,768]{1,0:T(8,128)(2,1)S(1)}, bf16[128,768]{1,0:T(8,128)(2,1)S(1)}, bf16[32,2,256]{2,1,0:T(2,128)(2,1)}) custom-call(s32[5]{0:T(128)S(1)} %stack.27.place_ref, bf16[128,768]{1,0:T(8,128)(2,1)S(1)} %tower.1.halved_ref, bf16[768,768]{1,0:T(8,128)(2,1)S(1)} %get-tuple-element.24.widen_ref, ...), custom_call_target="tpu_custom_call" | custom-call | flops 301989888 | bytes 4194304 | tf_op jit(solution)/shard_map/widen/pallas_call | solution.py:328
  11.2 0.1 collective-permute-start.4
  11.3 0.0 copy-done.1
  11.3 0.4 %collective-permute-start.3 = (bf16[3,3,64,128]{3,2,1,0:T(8,128)(2,1)S(1)}, bf16[3,3,64,128]{3,2,1,0:T(8,128)(2,1)S(1)}, u32[]{:S(2)}, u32[]{:S(2)}) collective-permute-start(bf16[3,3,64,128]{3,2,1,0:T(8,128)(2,1)S(1)} %bitcast.15), channel_id=1, source_target_pairs={{0,1},{1,0},{2,3},{3,2},{4,5},{5,4},{6,7},{7,6},{8,9},{9,8},{10,11... | collective-permute-start | bytes 442376 | tf_op jit(solution)/shard_map/ppermute | solution.py:32
  11.8 4.7 %all-to-all-start = ((bf16[32,2,256]{2,1,0:T(2,128)(2,1)}), bf16[32,2,256]{2,1,0:T(2,128)(2,1)S(1)}, u32[]{:S(2)}, u32[]{:S(2)}) async-start(bf16[32,2,256]{2,1,0:T(2,128)(2,1)} %get-tuple-element.27), calls=%async_computation | async-start | bytes 65536 | tf_op jit(solution)/shard_map/all_to_all | solution.py:552
  16.4 0.0 collective-permute-done.3.weight_other_ref
  16.5 7.2 %all-to-all-done.every_ref = bf16[32,2,256]{2,1,0:T(2,128)(2,1)S(1)} async-done(((bf16[32,2,256]{2,1,0:T(2,128)(2,1)}), bf16[32,2,256]{2,1,0:T(2,128)(2,1)S(1)}, u32[]{:S(2)}, u32[]{:S(2)}) %all-to-all-start) | async-done | bytes 32800 | tf_op jit(solution)/shard_map/all_to_all | solution.py:552
  23.7 0.0 collective-permute-done.4.fine_received_ref
  23.7 0.0 copy-done
  23.7 1.9 %pair.1 = (bf16[256,768]{1,0:T(8,128)(2,1)}, bf16[8,16,64]{2,1,0:T(8,128)(2,1)}) custom-call(s32[5]{0:T(128)S(1)} %stack.27.place_ref, bf16[32,2,256]{2,1,0:T(2,128)(2,1)S(1)} %all-to-all-done.every_ref, f32[1,128]{1,0:T(1,128)S(1)} %bitcast.12, bf16[3,3,64,128]{3,2,1,0:T(8,128)(2,1)S(1)} %get-tuple-element.28.weight_one_ref, ...), custom_call_target="tpu_custom_call" | custom-call | tf_op jit(solution)/shard_map/pair/pallas_call | solution.py:450
Async XLA Ops:
  0.6 6.8 %collective-permute-start.1 = (bf16[3,768,384]{2,1,0:T(8,128)(2,1)}, bf16[3,768,384]{2,1,0:T(8,128)(2,1)S(1)}, u32[]{:S(2)}, u32[]{:S(2)}) collective-permute-start(bf16[3,768,384]{2,1,0:T(8,128)(2,1)} %dilated_hbm.1), channel_id=1, source_target_pairs={{0,1},{1,0},{2,3},{3,2},{4,5},{5,4},{6,7},{7,6},{8,9},{9,8},{10,11... | collective-permute-start | bytes 5308424 | tf_op jit(solution)/shard_map/ppermute | solution.py:32
  1.2 8.0 %collective-permute-start.2 = (bf16[768,768]{1,0:T(8,128)(2,1)}, bf16[768,768]{1,0:T(8,128)(2,1)S(1)}, u32[]{:S(2)}, u32[]{:S(2)}) collective-permute-start(bf16[768,768]{1,0:T(8,128)(2,1)} %widen_hbm.1), channel_id=1, source_target_pairs={{0,1},{1,0},{2,3},{3,2},{4,5},{5,4},{6,7},{7,6},{8,9},{9,8},{10,11... | collective-permute-start | bytes 3538952 | tf_op jit(solution)/shard_map/ppermute | solution.py:32
  1.3 6.1 %collective-permute-start = (s32[64,128]{1,0:T(8,128)}, s32[64,128]{1,0:T(8,128)S(1)}, u32[]{:S(2)}, u32[]{:S(2)}) collective-permute-start(s32[64,128]{1,0:T(8,128)} %bitcast.16), channel_id=1, source_target_pairs={{1,2},{2,1},{3,4},{4,3},{5,6},{6,5},{7,8},{8,7},{9,10},{10,9},{11,... | collective-permute-start | bytes 98312 | tf_op jit(solution)/shard_map/ppermute | solution.py:499
  9.2 2.1 %copy-start.1 = (bf16[3,3,128,64]{2,3,1,0:T(8,128)(2,1)S(1)}, bf16[3,3,128,64]{2,3,1,0:T(8,128)(2,1)}, u32[]{:S(2)}) copy-start(bf16[3,3,128,64]{2,3,1,0:T(8,128)(2,1)} %param.18) | copy-start | bytes 442372
  9.2 14.5 %copy-start = (f32[128]{0:T(128)S(1)}, f32[128]{0:T(128)}, u32[]{:S(2)}) copy-start(f32[128]{0:T(128)} %param.17) | copy-start | bytes 1540
  11.2 12.5 %collective-permute-start.4 = (bf16[128,768]{1,0:T(8,128)(2,1)S(1)}, bf16[128,768]{1,0:T(8,128)(2,1)S(1)}, u32[]{:S(2)}, u32[]{:S(2)}) collective-permute-start(bf16[128,768]{1,0:T(8,128)(2,1)S(1)} %get-tuple-element.31), channel_id=1, source_target_pairs={{0,1},{1,0},{2,3},{3,2},{4,5},{5,4},{6,7},{7,6},{8,9},{9,8},{10,11... | collective-permute-start | bytes 589832 | tf_op jit(solution)/shard_map/ppermute | solution.py:32
  11.3 5.1 %collective-permute-start.3 = (bf16[3,3,64,128]{3,2,1,0:T(8,128)(2,1)S(1)}, bf16[3,3,64,128]{3,2,1,0:T(8,128)(2,1)S(1)}, u32[]{:S(2)}, u32[]{:S(2)}) collective-permute-start(bf16[3,3,64,128]{3,2,1,0:T(8,128)(2,1)S(1)} %bitcast.15), channel_id=1, source_target_pairs={{0,1},{1,0},{2,3},{3,2},{4,5},{5,4},{6,7},{7,6},{8,9},{9,8},{10,11... | collective-permute-start | bytes 442376 | tf_op jit(solution)/shard_map/ppermute | solution.py:32
  11.8 12.0 %all-to-all-start = ((bf16[32,2,256]{2,1,0:T(2,128)(2,1)}), bf16[32,2,256]{2,1,0:T(2,128)(2,1)S(1)}, u32[]{:S(2)}, u32[]{:S(2)}) async-start(bf16[32,2,256]{2,1,0:T(2,128)(2,1)} %get-tuple-element.27), calls=%async_computation | async-start | bytes 65536 | tf_op jit(solution)/shard_map/all_to_all | solution.py:552
